TPU v7x, 32 devices: a whole 2x2x4 slice. The times are simulated.
32 devices in a mesh: chan: 4 (over y, core), blk: 8 (over z, x).
Axes of the slice: x: 2, y: 2, z: 4, core: 2. Of those that a mesh axis runs over, the one named last changes fastest.
Arguments:
- comp_alms: float32 [3, 4, 8, 4096], P(None, None, 'blk', 'chan'), may hold values from -6 to 6
- legendre: bfloat16 [2, 8, 4096, 32], P(None, 'blk'), may hold values from -0.09375 to 0.09375
- inv_noise: float32 [4, 2, 32, 8192], P('chan', None, 'blk'), may hold values from 0.5 to 5
- beam_window: float32 [4, 4096], replicated, may hold values from 0.1 to 1
- mixing: float32 [4, 3], replicated, may hold values from 0.2 to 1.5
- channel_of: int32 [4], replicated, may hold values from 0 to 3, each once
- m_orders: int32 [8], replicated, may hold values from 0 to 4095, as said below
- cycle_of: int32 [32], replicated, may hold values from 0 to 31, each once
- cycle_pixels: int32 [32], replicated, may hold values from 4 to 8192, as said below
Outputs:
- normal_product: float32 [3, 4, 8, 4096], P(None, None, 'blk', 'chan')
Inputs may be any that keep to these rules, and one draw needn't show every extreme that they name: `m_orders`: the orders are distinct. `cycle_pixels`: each entry is 4 * min(h, 2048, 8192 - h) for some cycle number h of 1 to 8191; at least one entry equals 8192.
All inputs are finite; a program needn't handle non-finite values.
Results may differ from a plain program's by a relative error of at most 0.0022.
Values may be sent and summed in bfloat16 or wider, within the bound.
A program may use at most 128 MiB of HBM per device.

v0:
```python
import functools
import math

import jax
import jax.numpy as jnp
from jax import lax
from jax.experimental import pallas as pl
from jax.experimental.pallas import tpu as pltpu
from jax.sharding import PartitionSpec as P

F32 = jnp.float32
BF16 = jnp.bfloat16
LANES = 128
NT = (((1,), (1,)), ((), ()))
NN = (((1,), (0,)), ((), ()))


def iota(shape, dim):
    return lax.broadcasted_iota(jnp.int32, shape, dim)


def dot(left, right, dims):
    return lax.dot_general(left, right, dims, preferred_element_type=F32)


def exact_mod(value, modulus, inverse):
    rest = value - jnp.floor(value * inverse) * modulus
    rest = jnp.where(rest < 0, rest + modulus, rest)
    return jnp.where(rest >= modulus, rest - modulus, rest)


def kernel(
    chans, blks, alm_hbm, leg_hbm, inv_hbm, beam_hbm, mix_s, chan_s, order_s, cycle_s, pixel_s,
    cycle_row, out_ref, comp_v, leg_v, inv_v, beam_v, gain_v, slot_leg, phases, send1, recv1,
    send2, recv2, in_sem, send_sem, recv_sem,
):
    comps = comp_v.shape[0]
    shard = comp_v.shape[2]
    cycles = leg_v.shape[1] // 4
    slots = inv_v.shape[0] // 2
    width = inv_v.shape[1]
    rows = 4 * chans
    total = chans * blks
    me_c = lax.axis_index("chan")
    me_b = lax.axis_index("blk")
    first = pl.multiple_of(me_c * shard, shard)

    def peer(offset):
        return lax.rem(me_c + offset // blks, chans), lax.rem(me_b + offset % blks, blks)

    def each_peer(act):
        if total <= 64:
            for offset in range(1, total):
                act(offset)
        else:
            lax.fori_loop(1, total, lambda offset, carry: (act(offset), carry)[1], 0)

    barrier = pltpu.get_barrier_semaphore()

    def greet(offset):
        pl.semaphore_signal(
            barrier, inc=1, device_id=peer(offset), device_id_type=pl.DeviceIdType.MESH
        )

    loads = []

    def load(src, dst):
        copy = pltpu.make_async_copy(src, dst, in_sem.at[len(loads)])
        copy.start()
        loads.append(copy)

    for comp in range(comps):
        for part in range(4):
            for half in range(2):
                load(alm_hbm.at[comp, part], comp_v.at[comp, pl.ds(4 * half + part, 1), :])
    load(beam_hbm.at[:, pl.ds(first, shard)], beam_v)
    for kind in range(2):
        for part in range(4):
            load(
                leg_hbm.at[kind, 0, :, pl.ds(first, shard)],
                leg_v.at[kind, pl.ds(part * cycles, cycles), :],
            )
    early = len(loads)
    for stokes in range(2):
        load(inv_hbm.at[0, stokes], inv_v.at[pl.ds(stokes * slots, slots), :])
    each_peer(greet)
    for copy in loads[:early]:
        copy.wait()

    low_half = iota((8, 1), 0) < 4
    keep = (iota((1, shard), 1) + first >= order_s[me_b]).astype(F32)
    mix_cols = []
    alm_rows = []
    for pair in range(chans // 2):
        picked = [chan_s[2 * pair], chan_s[2 * pair + 1]]
        columns = [
            jnp.where(low_half, mix_s[picked[0], comp], mix_s[picked[1], comp])
            for comp in range(comps)
        ]
        mix_cols.append(columns)
        mixed = columns[0] * comp_v[0]
        for comp in range(1, comps):
            mixed = mixed + columns[comp] * comp_v[comp]
        beam = jnp.where(
            low_half, beam_v[pl.ds(picked[0], 1), :], beam_v[pl.ds(picked[1], 1), :]
        )
        gain = beam * keep
        gain_v[pl.ds(8 * pair, 8), :] = gain
        alm_rows.append(mixed * gain)
    alm = jnp.concatenate(alm_rows, axis=0).astype(BF16)
    plus = dot(alm, leg_v[0], NT)
    minus = dot(alm, leg_v[1], NT)
    row_part = iota(plus.shape, 0) % 4
    lane_part = iota(plus.shape, 1) // cycles
    outer = (lane_part == 0) | (lane_part == 3)
    signed = jnp.where(outer, -minus, minus)
    joined = jnp.where(lane_part == row_part, plus, 0.0) + jnp.where(
        lane_part == 3 - row_part, signed, 0.0
    )
    folded = joined
    for step in range(1, 4):
        folded = folded + pltpu.roll(joined, rows - step, 0)
    send1[...] = folded

    pl.semaphore_wait(barrier, total - 1)

    def scatter(src_of, dst, phase):
        def start(offset):
            dest_c, dest_b = peer(offset)
            pltpu.make_async_remote_copy(
                src_ref=src_of(dest_c, dest_b),
                dst_ref=dst.at[me_c, pl.ds(me_b, 1), :],
                send_sem=send_sem.at[phase, offset],
                recv_sem=recv_sem.at[phase],
                device_id=(dest_c, dest_b),
                device_id_type=pl.DeviceIdType.MESH,
            ).start()

        each_peer(start)
        pltpu.make_async_copy(
            src_of(me_c, me_b), dst.at[me_c, pl.ds(me_b, 1), :], recv_sem.at[phase]
        ).start()

    def arrived(dst, phase):
        pltpu.make_async_copy(dst, dst, recv_sem.at[phase]).wait()

    def sent(src_of, dst, phase):
        def finish(offset):
            dest_c, dest_b = peer(offset)
            pltpu.make_async_remote_copy(
                src_ref=src_of(dest_c, dest_b),
                dst_ref=dst.at[me_c, pl.ds(me_b, 1), :],
                send_sem=send_sem.at[phase, offset],
                recv_sem=recv_sem.at[phase],
                device_id=(dest_c, dest_b),
                device_id_type=pl.DeviceIdType.MESH,
            ).wait_send()

        each_peer(finish)

    def by_channel(dest_c, dest_b):
        return send1.at[pl.ds(4 * dest_c, 1), :]

    def by_order(dest_c, dest_b):
        return send2.at[pl.ds(dest_b, 1), :]

    scatter(by_channel, recv1, 0)

    own_cycles = [cycle_s[me_b * slots + slot] for slot in range(slots)]
    own_pixels = [pixel_s[cycle].astype(F32) for cycle in own_cycles]

    def by_slot(slot_index, values):
        result = jnp.where(slot_index == 0, values[0], values[slots - 1])
        for slot in range(1, slots - 1):
            result = jnp.where(slot_index == slot, values[slot], result)
        return result

    grid = (slots * blks, LANES)
    row = iota(grid, 0)
    lane = iota(grid, 1).astype(F32)
    pixels = by_slot(row // blks, own_pixels)
    orders = jnp.zeros(grid, F32)
    for order in range(blks):
        orders = jnp.where(row % blks == order, order_s[order].astype(F32), orders)
    modulus = 2.0 * pixels
    inverse = 1.0 / modulus
    scale = jnp.float32(math.pi) / pixels
    fine = exact_mod(orders * (2.0 * lane + 1.0), modulus, inverse) * scale
    stride = exact_mod(orders * (2.0 * LANES), modulus, inverse)
    coarse = exact_mod(stride * lane, modulus, inverse) * scale
    fine_cos, fine_sin = jnp.cos(fine), jnp.sin(fine)
    coarse_cos, coarse_sin = jnp.cos(coarse), jnp.sin(coarse)
    half = slots * blks
    for chunk in range(width // LANES):
        turn_cos = coarse_cos[:, chunk : chunk + 1]
        turn_sin = coarse_sin[:, chunk : chunk + 1]
        window = pl.ds(chunk * LANES, LANES)
        phases[pl.ds(0, half), window] = (turn_cos * fine_cos - turn_sin * fine_sin).astype(BF16)
        phases[pl.ds(half, half), window] = (turn_sin * fine_cos + turn_cos * fine_sin).astype(
            BF16
        )

    for copy in loads[early:]:
        copy.wait()
    row_pixels = by_slot(iota((2 * slots, 1), 0) % slots, own_pixels)
    row_inverse = 1.0 / row_pixels
    live = iota((2 * slots, width), 1).astype(F32) < row_pixels
    inv_v[...] = jnp.where(live, inv_v[...], 0.0) * row_inverse

    cycle_hot = (iota((cycles, cycles), 0) == cycle_row[...]).astype(BF16)
    to_row, to_col = iota((cycles, cycles), 0), iota((cycles, cycles), 1)
    reorder = ((to_row // blks == to_col % slots) & (to_row % blks == to_col // slots)).astype(
        F32
    ).astype(BF16)
    slot_hot = dot(reorder, cycle_hot, NT).astype(BF16)
    for kind in range(2):
        slot_leg[pl.ds(kind * cycles, cycles), :] = dot(
            slot_hot, leg_v[kind, pl.ds(0, cycles), :], NN
        ).astype(BF16)

    pick_shape = (2 * slots, 4 * cycles)
    pick_row, pick_lane = iota(pick_shape, 0), iota(pick_shape, 1)
    pick = (
        (pick_lane // (2 * cycles) == pick_row // slots)
        & (pick_lane % cycles == by_slot(pick_row % slots, own_cycles))
    ).astype(F32).astype(BF16)
    place_shape = (2 * slots, 2 * slots * rows)
    place_row, place_lane = iota(place_shape, 0), iota(place_shape, 1)
    lane_p = place_lane % 4
    lane_q = place_lane // rows
    twist = lane_q >= slots
    source_p = jnp.where(twist, 3 - lane_p, lane_p)
    fits = (
        ((place_lane // 4) % chans == me_c)
        & (lane_q % slots == place_row % slots)
        & (source_p // 2 == place_row // slots)
    )
    twist_sign = jnp.where(twist & ((lane_p == 0) | (lane_p == 3)), -1.0, 1.0)
    place = [
        jnp.where(fits & (source_p % 2 == part), twist_sign * (1.0 - 2.0 * part), 0.0).astype(BF16)
        for part in range(2)
    ]

    arrived(recv1, 0)
    coeffs = recv1[0]
    for chan in range(1, chans):
        coeffs = coeffs + recv1[chan]
    even = (iota(coeffs.shape, 1) // cycles) % 2 == 0
    real_block = jnp.where(even, coeffs, 0.0)
    imag_block = jnp.where(even, 0.0, -coeffs)
    spread = jnp.concatenate([real_block] * slots + [imag_block] * slots, axis=0).astype(BF16)
    stacked = dot(pick, spread, NT)
    own_block = (iota(stacked.shape, 1) // blks) % slots == iota(stacked.shape, 0) % slots
    stacked = jnp.where(own_block, stacked, 0.0).astype(BF16)

    piece = min(1024, width)
    grads = jnp.zeros((2 * half, 2 * slots), F32)
    for index in range(width // piece):
        window = pl.ds(index * piece, piece)
        table = phases[:, window]
        maps = dot(stacked, table, NN)
        weighted = (inv_v[:, window] * maps).astype(BF16)
        grads = grads + dot(table, weighted, NT)
    own_lane = (iota(grads.shape, 0) // blks) % slots == iota(grads.shape, 1) % slots
    grads = jnp.where(own_lane, grads, 0.0)
    placed = None
    for part in range(2):
        summed = grads[part * half : part * half + blks]
        for slot in range(1, slots):
            begin = part * half + slot * blks
            summed = summed + grads[begin : begin + blks]
        term = dot(summed.astype(BF16), place[part], NN)
        placed = term if placed is None else placed + term
    send2[...] = placed
    scatter(by_order, recv2, 1)
    sent(by_channel, recv1, 0)

    arrived(recv2, 1)
    returned = recv2[0]
    for chan in range(1, chans):
        returned = returned + recv2[chan]
    lanes = returned.shape[1]
    blocks = [returned] + [
        pltpu.roll(returned, lanes - index * rows, 1) for index in range(1, 2 * slots)
    ]
    turned = jnp.concatenate(blocks, axis=0)[:, : max(rows, LANES)].T
    alm_grads = dot(turned[:rows].astype(BF16), slot_leg[...], NN) * gain_v[...]
    for comp in range(comps):
        mixed = mix_cols[0][comp] * alm_grads[0:8]
        for pair in range(1, chans // 2):
            mixed = mixed + mix_cols[pair][comp] * alm_grads[8 * pair : 8 * pair + 8]
        out_ref[comp] = mixed[0:4] + mixed[4:8]
    sent(by_order, recv2, 1)


def body(
    chans, blks, comp_alms, legendre, inv_noise, beam_window, mixing, channel_of, m_orders,
    cycle_of, cycle_pixels,
):
    comps, parts, order_dev, shard = comp_alms.shape
    cycles = legendre.shape[3]
    chan_dev, stokes, slots, width = inv_noise.shape
    assert parts == 4 and stokes == 2 and order_dev == 1 and chan_dev == 1
    rows = 4 * chans
    any_space = pl.BlockSpec(memory_space=pl.ANY)
    scalars = pl.BlockSpec(memory_space=pltpu.SMEM)
    vector = pl.BlockSpec(memory_space=pltpu.VMEM)
    lanes2 = 2 * slots * rows
    result = pl.pallas_call(
        functools.partial(kernel, chans, blks),
        out_shape=jax.ShapeDtypeStruct((comps, 4, shard), F32),
        in_specs=[any_space] * 4 + [scalars] * 5 + [vector],
        out_specs=vector,
        scratch_shapes=[
            pltpu.VMEM((comps, 8, shard), F32),
            pltpu.VMEM((2, 4 * cycles, shard), BF16),
            pltpu.VMEM((2 * slots, width), F32),
            pltpu.VMEM((beam_window.shape[0], shard), F32),
            pltpu.VMEM((rows, shard), F32),
            pltpu.VMEM((2 * cycles, shard), BF16),
            pltpu.VMEM((2 * slots * blks, width), BF16),
            pltpu.VMEM((rows, 4 * cycles), F32),
            pltpu.VMEM((chans, blks, 4 * cycles), F32),
            pltpu.VMEM((blks, lanes2), F32),
            pltpu.VMEM((chans, blks, lanes2), F32),
            pltpu.SemaphoreType.DMA((comps * 8 + 11,)),
            pltpu.SemaphoreType.DMA((2, chans * blks)),
            pltpu.SemaphoreType.DMA((2,)),
        ],
        compiler_params=pltpu.CompilerParams(collective_id=0, has_side_effects=True),
        name="normal_product",
    )(
        comp_alms, jnp.swapaxes(legendre, 2, 3), inv_noise, beam_window, mixing, channel_of,
        m_orders, cycle_of, cycle_pixels, cycle_of.reshape(1, cycles),
    )
    return result.reshape(comp_alms.shape)


def solution(mesh):
    in_specs = (
        P(None, None, "blk", "chan"),
        P(None, "blk", None, None),
        P("chan", None, "blk", None),
        P(),
        P(),
        P(),
        P(),
        P(),
        P(),
    )
    out_specs = P(None, None, "blk", "chan")
    work = functools.partial(body, mesh.shape["chan"], mesh.shape["blk"])
    return jax.shard_map(work, mesh=mesh, in_specs=in_specs, out_specs=out_specs, check_vma=False)
```

profile of v0, /device:TPU:0, one launch (start us, length us, event | category | flops | bytes accessed | tf_op | source)
XLA Modules:
  0.0 21.1 jit_solution(14265215232850171823)
XLA Ops:
  0.0 19.7 %normal_product.1 = f32[3,4,1024]{2,1,0:T(4,128)} custom-call(f32[3,4,1,1024]{3,2,1,0:T(1,128)} %alm_hbm.1, bf16[2,1,32,4096]{3,2,1,0:T(8,128)(2,1)} %bitcast.3, f32[1,2,4,8192]{3,2,1,0:T(4,128)} %inv_hbm.1, f32[4,4096]{1,0:T(4,128)} %beam_hbm.1, f32[4,3]{1,0:T(4,128)} %mix_s.1, s32[4]{0:T(128)} %chan_s.1, s32[8]{0:T(128)} %order_s.1, s32[32]{0:T(128)} %cycle_s.1, ...), custom_call_target="tpu_custom_call" | custom-call | tf_op jit(solution)/shard_map/normal_product/pallas_call | solution.py:309
  19.7 1.5 %copy.10 = f32[3,4,1,1024]{3,2,1,0:T(1,128)} copy(f32[3,4,1,1024]{3,1,0,2:T(4,128)} %bitcast.4) | data formatting | bytes 98304 | tf_op jit(solution)/shard_map/reshape | solution.py:336
where the time goes:
time: 21.4 us; the launch traced here: 21.1 us
  Pallas kernels  19.7 us (92%)
  local copies, waits for them, and re-layouts  1.47 us (7%)
    pallas_call x1, Pallas kernels, body(): pl.pallas_call(functools.partial(kernel, chans, blks), out_shape=jax.Shap...  19.7 us
    reshape x1, local copies, waits for them, and re-layouts, body(): return result.reshape(comp_alms.shape)  1.47 us

commit v1 on v0

--- a/solution.py
+++ b/solution.py
@@ -30,9 +30,10 @@
 
 
 def kernel(
-    chans, blks, alm_hbm, leg_hbm, inv_hbm, beam_hbm, mix_s, chan_s, order_s, cycle_s, pixel_s,
-    cycle_row, out_ref, comp_v, leg_v, inv_v, beam_v, gain_v, slot_leg, phases, send1, recv1,
-    send2, recv2, in_sem, send_sem, recv_sem,
+    chans, blks, alm_hbm, leg_hbm, inv_hbm, beam_hbm, mix_hbm, chan_hbm, order_hbm, cycle_hbm,
+    pixel_hbm, cycle_row_hbm, out_ref, mix_s, chan_s, order_s, cycle_s, pixel_s, cycle_row, comp_v,
+    leg_v, inv_v, beam_v, gain_v, slot_leg, phases, send1, recv1, send2, recv2, in_sem, send_sem,
+    recv_sem,
 ):
     comps = comp_v.shape[0]
     shard = comp_v.shape[2]
@@ -62,6 +63,7 @@
             barrier, inc=1, device_id=peer(offset), device_id_type=pl.DeviceIdType.MESH
         )
 
+    each_peer(greet)
     loads = []
 
     def load(src, dst):
@@ -69,6 +71,11 @@
         copy.start()
         loads.append(copy)
 
+    for src, dst in (
+        (mix_hbm, mix_s), (chan_hbm, chan_s), (order_hbm, order_s), (cycle_hbm, cycle_s),
+        (pixel_hbm, pixel_s), (cycle_row_hbm, cycle_row),
+    ):
+        load(src, dst)
     for comp in range(comps):
         for part in range(4):
             for half in range(2):
@@ -83,7 +90,6 @@
     early = len(loads)
     for stokes in range(2):
         load(inv_hbm.at[0, stokes], inv_v.at[pl.ds(stokes * slots, slots), :])
-    each_peer(greet)
     for copy in loads[:early]:
         copy.wait()
 
@@ -303,15 +309,20 @@
     assert parts == 4 and stokes == 2 and order_dev == 1 and chan_dev == 1
     rows = 4 * chans
     any_space = pl.BlockSpec(memory_space=pl.ANY)
-    scalars = pl.BlockSpec(memory_space=pltpu.SMEM)
     vector = pl.BlockSpec(memory_space=pltpu.VMEM)
     lanes2 = 2 * slots * rows
     result = pl.pallas_call(
         functools.partial(kernel, chans, blks),
-        out_shape=jax.ShapeDtypeStruct((comps, 4, shard), F32),
-        in_specs=[any_space] * 4 + [scalars] * 5 + [vector],
+        out_shape=pltpu.VMEM((comps, 4, shard), F32),
+        in_specs=[any_space] * 10,
         out_specs=vector,
         scratch_shapes=[
+            pltpu.SMEM(mixing.shape, F32),
+            pltpu.SMEM(channel_of.shape, jnp.int32),
+            pltpu.SMEM(m_orders.shape, jnp.int32),
+            pltpu.SMEM(cycle_of.shape, jnp.int32),
+            pltpu.SMEM(cycle_pixels.shape, jnp.int32),
+            pltpu.VMEM((1, cycles), jnp.int32),
             pltpu.VMEM((comps, 8, shard), F32),
             pltpu.VMEM((2, 4 * cycles, shard), BF16),
             pltpu.VMEM((2 * slots, width), F32),
@@ -323,7 +334,7 @@
             pltpu.VMEM((chans, blks, 4 * cycles), F32),
             pltpu.VMEM((blks, lanes2), F32),
             pltpu.VMEM((chans, blks, lanes2), F32),
-            pltpu.SemaphoreType.DMA((comps * 8 + 11,)),
+            pltpu.SemaphoreType.DMA((comps * 8 + 17,)),
             pltpu.SemaphoreType.DMA((2, chans * blks)),
             pltpu.SemaphoreType.DMA((2,)),
         ],

time: 21.4 us -> 19.1 us (0.89)
  Pallas kernels: 19.7 us -> 18.2 us
  local copies, waits for them, and re-layouts: 1.47 us -> 0.67 us
    pallas_call x1, Pallas kernels: 19.7 us -> 18.2 us  [body(): pl.pallas_call(functools.partial(kernel, chans, blks), out_shape=pltpu.VM...]
    reshape x1, local copies, waits for them, and re-layouts: 1.47 us -> 0.67 us  [body(): return result.reshape(comp_alms.shape)]
where the time goes in v1:
time: 19.1 us; the launch traced here: 18.9 us
  Pallas kernels  18.2 us (95%)
  local copies, waits for them, and re-layouts  0.67 us (4%)
    pallas_call x1, Pallas kernels, body(): pl.pallas_call(functools.partial(kernel, chans, blks), out_shape=pltpu.VM...  18.2 us
    reshape x1, local copies, waits for them, and re-layouts, body(): return result.reshape(comp_alms.shape)  0.67 us

profile of v1, /device:TPU:0, one launch (start us, length us, event | category | flops | bytes accessed | tf_op | source)
XLA Modules:
  0.0 18.9 jit_solution(5475636240847821466)
XLA Ops:
  0.0 18.2 %normal_product.1 = f32[3,4,1024]{2,1,0:T(4,128)S(1)} custom-call(f32[3,4,1,1024]{3,2,1,0:T(1,128)} %alm_hbm.1, bf16[2,1,32,4096]{3,2,1,0:T(8,128)(2,1)} %bitcast.4, f32[1,2,4,8192]{3,2,1,0:T(4,128)} %inv_hbm.1, f32[4,4096]{1,0:T(4,128)} %beam_hbm.1, f32[4,3]{1,0:T(4,128)} %mix_hbm.1, s32[4]{0:T(128)} %chan_hbm.1, s32[8]{0:T(128)} %order_hbm.1, ...), custom_call_target="tpu_custom_call" | custom-call | tf_op jit(solution)/shard_map/normal_product/pallas_call | solution.py:314
  18.2 0.7 %copy.10 = f32[3,4,1,1024]{3,2,1,0:T(1,128)} copy(f32[3,4,1,1024]{3,1,0,2:T(4,128)S(1)} %bitcast.3) | data formatting | bytes 98304 | tf_op jit(solution)/shard_map/reshape | solution.py:347

commit v2 on v1

--- a/solution.py
+++ b/solution.py
@@ -32,7 +32,7 @@
 def kernel(
     chans, blks, alm_hbm, leg_hbm, inv_hbm, beam_hbm, mix_hbm, chan_hbm, order_hbm, cycle_hbm,
     pixel_hbm, cycle_row_hbm, out_ref, mix_s, chan_s, order_s, cycle_s, pixel_s, cycle_row, comp_v,
-    leg_v, inv_v, beam_v, gain_v, slot_leg, phases, send1, recv1, send2, recv2, in_sem, send_sem,
+    leg_v, inv_v, beam_v, gain_v, slot_leg, phases, send1, recv1, send2, recv2, spare, in_sem, send_sem,
     recv_sem,
 ):
     comps = comp_v.shape[0]
@@ -64,34 +64,40 @@
         )
 
     each_peer(greet)
-    loads = []
-
-    def load(src, dst):
-        copy = pltpu.make_async_copy(src, dst, in_sem.at[len(loads)])
+    scalars = []
+
+    def load(src, dst, group):
+        copy = pltpu.make_async_copy(src, dst, in_sem.at[group])
         copy.start()
-        loads.append(copy)
+        return copy
+
+    def loaded(dst, group):
+        pltpu.make_async_copy(dst, dst, in_sem.at[group]).wait()
 
     for src, dst in (
         (mix_hbm, mix_s), (chan_hbm, chan_s), (order_hbm, order_s), (cycle_hbm, cycle_s),
         (pixel_hbm, pixel_s), (cycle_row_hbm, cycle_row),
     ):
-        load(src, dst)
+        scalars.append(load(src, dst, 4 + len(scalars)))
     for comp in range(comps):
         for part in range(4):
             for half in range(2):
-                load(alm_hbm.at[comp, part], comp_v.at[comp, pl.ds(4 * half + part, 1), :])
-    load(beam_hbm.at[:, pl.ds(first, shard)], beam_v)
+                load(alm_hbm.at[comp, part], comp_v.at[comp, pl.ds(4 * half + part, 1), :], 0)
+    load(beam_hbm.at[:, pl.ds(first, shard)], beam_v, 1)
     for kind in range(2):
         for part in range(4):
             load(
                 leg_hbm.at[kind, 0, :, pl.ds(first, shard)],
                 leg_v.at[kind, pl.ds(part * cycles, cycles), :],
+                2,
             )
-    early = len(loads)
     for stokes in range(2):
-        load(inv_hbm.at[0, stokes], inv_v.at[pl.ds(stokes * slots, slots), :])
-    for copy in loads[:early]:
+        load(inv_hbm.at[0, stokes], inv_v.at[pl.ds(stokes * slots, slots), :], 3)
+    for copy in scalars:
         copy.wait()
+    loaded(comp_v, 0)
+    loaded(beam_v, 1)
+    loaded(leg_v, 2)
 
     low_half = iota((8, 1), 0) < 4
     keep = (iota((1, shard), 1) + first >= order_s[me_b]).astype(F32)
@@ -136,7 +142,7 @@
             pltpu.make_async_remote_copy(
                 src_ref=src_of(dest_c, dest_b),
                 dst_ref=dst.at[me_c, pl.ds(me_b, 1), :],
-                send_sem=send_sem.at[phase, offset],
+                send_sem=send_sem.at[phase],
                 recv_sem=recv_sem.at[phase],
                 device_id=(dest_c, dest_b),
                 device_id_type=pl.DeviceIdType.MESH,
@@ -146,23 +152,13 @@
         pltpu.make_async_copy(
             src_of(me_c, me_b), dst.at[me_c, pl.ds(me_b, 1), :], recv_sem.at[phase]
         ).start()
+        pltpu.make_async_copy(src_of(me_c, me_b), spare.at[phase], send_sem.at[phase]).start()
 
     def arrived(dst, phase):
         pltpu.make_async_copy(dst, dst, recv_sem.at[phase]).wait()
 
-    def sent(src_of, dst, phase):
-        def finish(offset):
-            dest_c, dest_b = peer(offset)
-            pltpu.make_async_remote_copy(
-                src_ref=src_of(dest_c, dest_b),
-                dst_ref=dst.at[me_c, pl.ds(me_b, 1), :],
-                send_sem=send_sem.at[phase, offset],
-                recv_sem=recv_sem.at[phase],
-                device_id=(dest_c, dest_b),
-                device_id_type=pl.DeviceIdType.MESH,
-            ).wait_send()
-
-        each_peer(finish)
+    def sent(dst, phase):
+        pltpu.make_async_copy(dst, dst, send_sem.at[phase]).wait()
 
     def by_channel(dest_c, dest_b):
         return send1.at[pl.ds(4 * dest_c, 1), :]
@@ -206,8 +202,7 @@
             BF16
         )
 
-    for copy in loads[early:]:
-        copy.wait()
+    loaded(inv_v, 3)
     row_pixels = by_slot(iota((2 * slots, 1), 0) % slots, own_pixels)
     row_inverse = 1.0 / row_pixels
     live = iota((2 * slots, width), 1).astype(F32) < row_pixels
@@ -279,7 +274,7 @@
         placed = term if placed is None else placed + term
     send2[...] = placed
     scatter(by_order, recv2, 1)
-    sent(by_channel, recv1, 0)
+    sent(recv1, 0)
 
     arrived(recv2, 1)
     returned = recv2[0]
@@ -296,7 +291,7 @@
         for pair in range(1, chans // 2):
             mixed = mixed + mix_cols[pair][comp] * alm_grads[8 * pair : 8 * pair + 8]
         out_ref[comp] = mixed[0:4] + mixed[4:8]
-    sent(by_order, recv2, 1)
+    sent(recv2, 1)
 
 
 def body(
@@ -311,6 +306,7 @@
     any_space = pl.BlockSpec(memory_space=pl.ANY)
     vector = pl.BlockSpec(memory_space=pltpu.VMEM)
     lanes2 = 2 * slots * rows
+    assert lanes2 == 4 * cycles
     result = pl.pallas_call(
         functools.partial(kernel, chans, blks),
         out_shape=pltpu.VMEM((comps, 4, shard), F32),
@@ -334,8 +330,9 @@
             pltpu.VMEM((chans, blks, 4 * cycles), F32),
             pltpu.VMEM((blks, lanes2), F32),
             pltpu.VMEM((chans, blks, lanes2), F32),
-            pltpu.SemaphoreType.DMA((comps * 8 + 17,)),
-            pltpu.SemaphoreType.DMA((2, chans * blks)),
+            pltpu.VMEM((2, 1, 4 * cycles), F32),
+            pltpu.SemaphoreType.DMA((10,)),
+            pltpu.SemaphoreType.DMA((2,)),
             pltpu.SemaphoreType.DMA((2,)),
         ],
         compiler_params=pltpu.CompilerParams(collective_id=0, has_side_effects=True),

time: 19.1 us -> 18.2 us (0.953)
  Pallas kernels: 18.2 us -> 17.3 us
    pallas_call x1, Pallas kernels: 18.2 us -> 17.3 us  [body(): pl.pallas_call(functools.partial(kernel, chans, blks), out_shape=pltpu.VM...]
where the time goes in v2:
time: 18.2 us; the launch traced here: 18 us
  Pallas kernels  17.3 us (95%)
  local copies, waits for them, and re-layouts  0.67 us (4%)
    pallas_call x1, Pallas kernels, body(): pl.pallas_call(functools.partial(kernel, chans, blks), out_shape=pltpu.VM...  17.3 us
    reshape x1, local copies, waits for them, and re-layouts, body(): return result.reshape(comp_alms.shape)  0.67 us

profile of v2, /device:TPU:0, one launch (start us, length us, event | category | flops | bytes accessed | tf_op | source)
XLA Modules:
  0.0 18.0 jit_solution(15040415871502460994)
XLA Ops:
  0.0 17.3 %normal_product.1 = f32[3,4,1024]{2,1,0:T(4,128)S(1)} custom-call(f32[3,4,1,1024]{3,2,1,0:T(1,128)} %alm_hbm.1, bf16[2,1,32,4096]{3,2,1,0:T(8,128)(2,1)} %bitcast.4, f32[1,2,4,8192]{3,2,1,0:T(4,128)} %inv_hbm.1, f32[4,4096]{1,0:T(4,128)} %beam_hbm.1, f32[4,3]{1,0:T(4,128)} %mix_hbm.1, s32[4]{0:T(128)} %chan_hbm.1, s32[8]{0:T(128)} %order_hbm.1, ...), custom_call_target="tpu_custom_call" | custom-call | tf_op jit(solution)/shard_map/normal_product/pallas_call | solution.py:310
  17.4 0.7 %copy.10 = f32[3,4,1,1024]{3,2,1,0:T(1,128)} copy(f32[3,4,1,1024]{3,1,0,2:T(4,128)S(1)} %bitcast.3) | data formatting | bytes 98304 | tf_op jit(solution)/shard_map/reshape | solution.py:344
